TPU v7x, 32 devices: a whole 2x2x4 slice. The times are simulated.
32 devices in a mesh: gy: 4 (over y, core), gx: 8 (over z, x).
Axes of the slice: x: 2, y: 2, z: 4, core: 2. Of those that a mesh axis runs over, the one named last changes fastest.
Arguments:
- phase: float32 [2, 128, 1024], P(None, 'gy', 'gx'), may hold values from -1.5 to 1.5
- velocity: float32 [2, 128, 1024], P(None, 'gy', 'gx'), may hold values from -2 to 2
- offsets: int32 [2, 4], replicated, may hold values from 0 to 1020, as said below
Outputs:
- phase_out: float32 [2, 128, 1024], P(None, 'gy', 'gx')
Inputs may be any that keep to these rules, and one draw needn't show every extreme that they name: `offsets`: every offset is a multiple of 2 ** 2.
All inputs are finite; a program needn't handle non-finite values.
Results may differ from a plain program's by a relative error of at most 0.00014.
Values sent between devices are 32-bit elements; how exact they have to be, the bound alone decides.
No kernel may reach another device: no remote copies, remote signals or barrier semaphores. Data moves between devices by JAX's collectives and lax.ppermute only.
A program may use at most 64 MiB of HBM per device.

v0:
```python
import jax
import jax.numpy as jnp
from jax import lax
from jax.sharding import PartitionSpec as P

STEPS = 2
ITERS = 2
LEVELS = 3
COARSE = 4
RELAXATION = 0.8
DIFFUSION = 4.0
VERTICAL = 1.0
REACTION = 0.5
ADVECTION = 0.5


def padded(cells, sides, width):
    for axis, dim in sides:
        count = lax.axis_size(axis)
        head = lax.slice_in_dim(cells, 0, width, axis=dim)
        tail = lax.slice_in_dim(cells, cells.shape[dim] - width, cells.shape[dim], axis=dim)
        cells = jnp.concatenate(
            [
                lax.ppermute(tail, axis, [(i, (i + 1) % count) for i in range(count)]),
                cells,
                lax.ppermute(head, axis, [((i + 1) % count, i) for i in range(count)]),
            ],
            axis=dim,
        )
    return cells


def sheared(bottom_row, upper_row, offsets_now, anchor, columns):
    breadth = bottom_row.shape[1]
    device_row = lax.axis_index("gy")
    row_count = lax.axis_size("gy")
    below_shift = offsets_now[device_row]
    above_shift = offsets_now[(device_row + 1) % row_count]
    local_columns = jnp.arange(columns, dtype=jnp.int32)
    down_index = (anchor + below_shift + local_columns) % breadth
    up_index = (anchor - above_shift + local_columns) % breadth
    down_window = jnp.take(bottom_row, down_index, axis=1)
    up_window = jnp.take(upper_row, up_index, axis=1)
    stacked = jnp.stack([down_window, up_window], axis=1)
    rims = padded(stacked, (("gy", 1),), 1)
    return (rims[:, 0, :], rims[:, 3, :])


def stencil(field, below_row, above_row, across, coupling):
    diagonal = 1.0 + 4.0 * coupling + 2.0 * VERTICAL
    column_pad = jnp.concatenate([below_row[:, None, :], field, above_row[:, None, :]], axis=1)
    beside = column_pad[:, 2:, :] + column_pad[:, :-2, :] + across
    vertical_sum = jnp.roll(field, 1, 0) + jnp.roll(field, -1, 0)
    return diagonal * field - coupling * beside - VERTICAL * vertical_sum


def operate(field, offsets_now, coupling):
    columns = field.shape[2]
    margins = padded(field, (("gx", 2),), 1)
    bottom_full, upper_full = (
        lax.all_gather(field[:, 0, :], "gx", axis=1, tiled=True),
        lax.all_gather(field[:, -1, :], "gx", axis=1, tiled=True),
    )
    right_field = margins[:, :, 2:]
    left_field = margins[:, :, :-2]
    below_row, above_row = sheared(
        bottom_full, upper_full, offsets_now, lax.axis_index("gx") * columns, columns
    )
    across = right_field + left_field
    return (stencil(field, below_row, above_row, across, coupling), right_field, left_field)


def operate_strip(field, offsets_now, coupling):
    below_row, above_row = sheared(field[:, 0, :], field[:, -1, :], offsets_now, 0, field.shape[2])
    across = jnp.roll(field, 1, 2) + jnp.roll(field, -1, 2)
    return stencil(field, below_row, above_row, across, coupling)


def coarsest(residual, offsets_now, coupling):
    diagonal = 1.0 + 4.0 * coupling + 2.0 * VERTICAL
    columns = residual.shape[2]
    gathered = lax.all_gather(residual, "gx", axis=2, tiled=True)
    estimate = RELAXATION * gathered / diagonal
    for sweep_index in range(COARSE - 1):
        estimate = (
            estimate
            + RELAXATION * (gathered - operate_strip(estimate, offsets_now, coupling)) / diagonal
        )
    return lax.dynamic_slice_in_dim(estimate, lax.axis_index("gx") * columns, columns, 2)


def vcycle(residual, offsets_raw, layer_index):
    factor = 2**layer_index
    coupling = DIFFUSION / 4.0**layer_index
    diagonal = 1.0 + 4.0 * coupling + 2.0 * VERTICAL
    offsets_now = offsets_raw // factor
    if layer_index == LEVELS - 1:
        return coarsest(residual, offsets_now, coupling)
    estimate = RELAXATION * residual / diagonal
    defect = residual - operate(estimate, offsets_now, coupling)[0]
    planes, height, breadth = defect.shape
    coarser = defect.reshape(planes, height // 2, 2, breadth // 2, 2).mean(axis=(2, 4))
    correction = vcycle(coarser, offsets_raw, layer_index + 1)
    estimate = estimate + jnp.repeat(jnp.repeat(correction, 2, axis=1), 2, axis=2)
    estimate = (
        estimate + RELAXATION * (residual - operate(estimate, offsets_now, coupling)[0]) / diagonal
    )
    return estimate


def total_inner(first_field, second_field):
    return lax.psum(jnp.sum(first_field * second_field), ("gy", "gx"))


def local(phase, velocity, offsets):
    phase_now = phase
    for time_step in range(STEPS):
        offsets_raw = offsets[time_step]
        applied, right_field, left_field = operate(phase_now, offsets_raw, DIFFUSION)
        source = (
            phase_now
            + REACTION * (phase_now - phase_now * phase_now * phase_now)
            - ADVECTION * velocity * (right_field - left_field)
        )
        residual = source - applied
        precond = vcycle(residual, offsets_raw, 0)
        projected = total_inner(residual, precond)
        direction = precond
        for iteration in range(ITERS):
            image = operate(direction, offsets_raw, DIFFUSION)[0]
            step_size = projected / total_inner(direction, image)
            phase_now = phase_now + step_size * direction
            residual = residual - step_size * image
            if iteration + 1 < ITERS:
                precond = vcycle(residual, offsets_raw, 0)
                following = total_inner(residual, precond)
                direction = precond + following / projected * direction
                projected = following
    return phase_now


def solution(mesh):
    placed = (P(None, "gy", "gx"), P(None, "gy", "gx"), P())
    return jax.shard_map(
        local, mesh=mesh, in_specs=placed, out_specs=P(None, "gy", "gx"), check_vma=False
    )
```

profile of v0, /device:TPU:12, one launch (start us, length us, event | category | flops | bytes accessed | tf_op | source)
XLA Modules:
  0.0 1669.2 jit_solution(4805464784161272798)
XLA Ops:
  6.4 31.0 %all-gather.1 = f32[2,1,1024]{0,2,1:T(8,128)S(1)} all-gather(f32[2,1,128]{0,2,1:T(8,128)S(1)} %copy.2969), channel_id=3, replica_groups=mesh['gy'=4,'gx'=8] {'gx'}, dimensions={2}, use_global_device_ids=true | all-gather | bytes 9216 | tf_op jit(solution)/shard_map/all_gather | solution.py:62
  38.3 31.4 %all-gather = f32[2,1,1024]{0,2,1:T(8,128)S(1)} all-gather(f32[2,1,128]{0,2,1:T(8,128)S(1)} %copy.2968), channel_id=2, replica_groups=mesh['gy'=4,'gx'=8] {'gx'}, dimensions={2}, use_global_device_ids=true | all-gather | bytes 9216 | tf_op jit(solution)/shard_map/all_gather | solution.py:61
  83.4 20.7 %all-gather.2 = f32[2,1,1024]{2,1,0:T(1,128)S(1)} all-gather(f32[2,1,128]{2,1,0:T(1,128)S(1)} %get-tuple-element.104), channel_id=4, replica_groups=mesh['gy'=4,'gx'=8] {'gx'}, dimensions={2}, use_global_device_ids=true | all-gather | bytes 9216 | tf_op jit(solution)/shard_map/all_gather | solution.py:61
  104.1 16.3 all-gather.3
  135.9 29.8 %all-gather.5 = f32[2,1,512]{0,1,2:T(1,128)S(1)} all-gather(f32[2,1,64]{0,1,2:T(1,128)S(1)} %copy.2705), channel_id=7, replica_groups=mesh['gy'=4,'gx'=8] {'gx'}, dimensions={2}, use_global_device_ids=true | all-gather | bytes 4608 | tf_op jit(solution)/shard_map/all_gather | solution.py:62
  166.5 30.8 %all-gather.4 = f32[2,1,512]{0,1,2:T(1,128)S(1)} all-gather(f32[2,1,64]{0,1,2:T(1,128)S(1)} %copy.2702), channel_id=6, replica_groups=mesh['gy'=4,'gx'=8] {'gx'}, dimensions={2}, use_global_device_ids=true | all-gather | bytes 4608 | tf_op jit(solution)/shard_map/all_gather | solution.py:61
  200.2 30.9 %all_gather.150 = f32[2,8,256]{1,0,2:T(2,128)S(1)} all-gather(f32[2,8,32]{1,0,2:T(2,128)S(1)} %copy.2708), channel_id=1, replica_groups=mesh['gy'=4,'gx'=8] {'gx'}, dimensions={2}, use_global_device_ids=true | all-gather | bytes 18432 | tf_op jit(solution)/shard_map/all_gather | solution.py:82
  252.2 30.9 %all-gather.7 = f32[2,1,512]{0,1,2:T(1,128)S(1)} all-gather(f32[2,1,64]{0,1,2:T(1,128)S(1)} %copy.2731), channel_id=9, replica_groups=mesh['gy'=4,'gx'=8] {'gx'}, dimensions={2}, use_global_device_ids=true | all-gather | bytes 4608 | tf_op jit(solution)/shard_map/all_gather | solution.py:62
  283.9 30.9 %all-gather.6 = f32[2,1,512]{0,1,2:T(1,128)S(1)} all-gather(f32[2,1,64]{0,1,2:T(1,128)S(1)} %copy.2728), channel_id=8, replica_groups=mesh['gy'=4,'gx'=8] {'gx'}, dimensions={2}, use_global_device_ids=true | all-gather | bytes 4608 | tf_op jit(solution)/shard_map/all_gather | solution.py:61
  317.2 20.7 %all-gather.8 = f32[2,1,1024]{2,1,0:T(1,128)S(1)} all-gather(f32[2,1,128]{2,1,0:T(1,128)S(1)} %get-tuple-element.98), channel_id=10, replica_groups=mesh['gy'=4,'gx'=8] {'gx'}, dimensions={2}, use_global_device_ids=true | all-gather | bytes 9216 | tf_op jit(solution)/shard_map/all_gather | solution.py:61
  337.9 16.3 all-gather.9
  364.1 18.3 %all-gather.10 = f32[2,1,1024]{2,1,0:T(1,128)S(1)} all-gather(f32[2,1,128]{2,1,0:T(1,128)S(1)} %get-tuple-element.90), channel_id=12, replica_groups=mesh['gy'=4,'gx'=8] {'gx'}, dimensions={2}, use_global_device_ids=true | all-gather | bytes 9216 | tf_op jit(solution)/shard_map/all_gather | solution.py:61
  382.4 16.3 all-gather.11
  409.6 42.1 %all-reduce.1 = (f32[]{:T(128)}, f32[]{:T(128)}) all-reduce(f32[]{:T(128)} %get-tuple-element.11, f32[]{:T(128)} %get-tuple-element.10), channel_id=1, replica_groups=mesh['gy'=4,'gx'=8] {'gy','gx'}, use_global_device_ids=true, to_apply=%region_3.7 | all-reduce | flops 2 | bytes 16 | tf_op jit(solution)/shard_map/psum | solution.py:112
  467.8 16.5 all-gather.13
  499.5 29.8 %all-gather.15 = f32[2,1,512]{0,1,2:T(1,128)S(1)} all-gather(f32[2,1,64]{0,1,2:T(1,128)S(1)} %copy.2751), channel_id=17, replica_groups=mesh['gy'=4,'gx'=8] {'gx'}, dimensions={2}, use_global_device_ids=true | all-gather | bytes 4608 | tf_op jit(solution)/shard_map/all_gather | solution.py:62
  530.1 30.7 %all-gather.14 = f32[2,1,512]{0,1,2:T(1,128)S(1)} all-gather(f32[2,1,64]{0,1,2:T(1,128)S(1)} %copy.2748), channel_id=16, replica_groups=mesh['gy'=4,'gx'=8] {'gx'}, dimensions={2}, use_global_device_ids=true | all-gather | bytes 4608 | tf_op jit(solution)/shard_map/all_gather | solution.py:61
  563.8 30.8 %all_gather.161 = f32[2,8,256]{1,0,2:T(2,128)S(1)} all-gather(f32[2,8,32]{1,0,2:T(2,128)S(1)} %copy.2754), channel_id=1, replica_groups=mesh['gy'=4,'gx'=8] {'gx'}, dimensions={2}, use_global_device_ids=true | all-gather | bytes 18432 | tf_op jit(solution)/shard_map/all_gather | solution.py:82
  616.1 30.9 %all-gather.17 = f32[2,1,512]{0,1,2:T(1,128)S(1)} all-gather(f32[2,1,64]{0,1,2:T(1,128)S(1)} %copy.2777), channel_id=19, replica_groups=mesh['gy'=4,'gx'=8] {'gx'}, dimensions={2}, use_global_device_ids=true | all-gather | bytes 4608 | tf_op jit(solution)/shard_map/all_gather | solution.py:62
  647.8 30.8 %all-gather.16 = f32[2,1,512]{0,1,2:T(1,128)S(1)} all-gather(f32[2,1,64]{0,1,2:T(1,128)S(1)} %copy.2774), channel_id=18, replica_groups=mesh['gy'=4,'gx'=8] {'gx'}, dimensions={2}, use_global_device_ids=true | all-gather | bytes 4608 | tf_op jit(solution)/shard_map/all_gather | solution.py:61
  681.1 20.7 %all-gather.18 = f32[2,1,1024]{2,1,0:T(1,128)S(1)} all-gather(f32[2,1,128]{2,1,0:T(1,128)S(1)} %get-tuple-element.78), channel_id=20, replica_groups=mesh['gy'=4,'gx'=8] {'gx'}, dimensions={2}, use_global_device_ids=true | all-gather | bytes 9216 | tf_op jit(solution)/shard_map/all_gather | solution.py:61
  701.8 16.3 all-gather.19
  728.5 42.0 %psum.58 = f32[]{:T(128)} all-reduce(f32[]{:T(128)} %get-tuple-element.23), channel_id=1, replica_groups=mesh['gy'=4,'gx'=8] {'gy','gx'}, use_global_device_ids=true, to_apply=%region_9.13 | all-reduce | flops 1 | bytes 8 | tf_op jit(solution)/shard_map/psum | solution.py:112
  786.6 16.6 all-gather.21
  813.3 42.1 %psum.59 = f32[]{:T(128)} all-reduce(f32[]{:T(128)} %fusion.65), channel_id=1, replica_groups=mesh['gy'=4,'gx'=8] {'gy','gx'}, use_global_device_ids=true, to_apply=%region_11.15 | all-reduce | flops 1 | bytes 8 | tf_op jit(solution)/shard_map/psum | solution.py:112
  871.8 16.3 all-gather.23
  898.0 18.3 %all-gather.24 = f32[2,1,1024]{2,1,0:T(1,128)S(1)} all-gather(f32[2,1,128]{2,1,0:T(1,128)S(1)} %get-tuple-element.62), channel_id=26, replica_groups=mesh['gy'=4,'gx'=8] {'gx'}, dimensions={2}, use_global_device_ids=true | all-gather | bytes 9216 | tf_op jit(solution)/shard_map/all_gather | solution.py:61
  948.0 29.8 %all-gather.27 = f32[2,1,512]{0,1,2:T(1,128)S(1)} all-gather(f32[2,1,64]{0,1,2:T(1,128)S(1)} %copy.2801), channel_id=29, replica_groups=mesh['gy'=4,'gx'=8] {'gx'}, dimensions={2}, use_global_device_ids=true | all-gather | bytes 4608 | tf_op jit(solution)/shard_map/all_gather | solution.py:62
  978.6 30.8 %all-gather.26 = f32[2,1,512]{0,1,2:T(1,128)S(1)} all-gather(f32[2,1,64]{0,1,2:T(1,128)S(1)} %copy.2798), channel_id=28, replica_groups=mesh['gy'=4,'gx'=8] {'gx'}, dimensions={2}, use_global_device_ids=true | all-gather | bytes 4608 | tf_op jit(solution)/shard_map/all_gather | solution.py:61
  1012.3 30.9 %all_gather.174 = f32[2,8,256]{1,0,2:T(2,128)S(1)} all-gather(f32[2,8,32]{1,0,2:T(2,128)S(1)} %copy.2804), channel_id=1, replica_groups=mesh['gy'=4,'gx'=8] {'gx'}, dimensions={2}, use_global_device_ids=true | all-gather | bytes 18432 | tf_op jit(solution)/shard_map/all_gather | solution.py:82
  1064.4 30.9 %all-gather.29 = f32[2,1,512]{0,1,2:T(1,128)S(1)} all-gather(f32[2,1,64]{0,1,2:T(1,128)S(1)} %copy.2827), channel_id=31, replica_groups=mesh['gy'=4,'gx'=8] {'gx'}, dimensions={2}, use_global_device_ids=true | all-gather | bytes 4608 | tf_op jit(solution)/shard_map/all_gather | solution.py:62
  1096.0 30.8 %all-gather.28 = f32[2,1,512]{0,1,2:T(1,128)S(1)} all-gather(f32[2,1,64]{0,1,2:T(1,128)S(1)} %copy.2824), channel_id=30, replica_groups=mesh['gy'=4,'gx'=8] {'gx'}, dimensions={2}, use_global_device_ids=true | all-gather | bytes 4608 | tf_op jit(solution)/shard_map/all_gather | solution.py:61
  1129.3 20.7 %all-gather.30 = f32[2,1,1024]{2,1,0:T(1,128)S(1)} all-gather(f32[2,1,128]{2,1,0:T(1,128)S(1)} %get-tuple-element.56), channel_id=32, replica_groups=mesh['gy'=4,'gx'=8] {'gx'}, dimensions={2}, use_global_device_ids=true | all-gather | bytes 9216 | tf_op jit(solution)/shard_map/all_gather | solution.py:61
  1150.1 16.3 all-gather.31
  1176.3 18.3 %all-gather.32 = f32[2,1,1024]{2,1,0:T(1,128)S(1)} all-gather(f32[2,1,128]{2,1,0:T(1,128)S(1)} %get-tuple-element.48), channel_id=34, replica_groups=mesh['gy'=4,'gx'=8] {'gx'}, dimensions={2}, use_global_device_ids=true | all-gather | bytes 9216 | tf_op jit(solution)/shard_map/all_gather | solution.py:61
  1194.6 16.3 all-gather.33
  1221.2 42.3 %all-reduce = (f32[]{:T(128)}, f32[]{:T(128)}) all-reduce(f32[]{:T(128)} %get-tuple-element.8, f32[]{:T(128)} %get-tuple-element.6), channel_id=1, replica_groups=mesh['gy'=4,'gx'=8] {'gy','gx'}, use_global_device_ids=true, to_apply=%region_15.19 | all-reduce | flops 2 | bytes 16 | tf_op jit(solution)/shard_map/psum | solution.py:112
  1279.6 16.6 all-gather.35
  1311.4 29.9 %all-gather.37 = f32[2,1,512]{0,1,2:T(1,128)S(1)} all-gather(f32[2,1,64]{0,1,2:T(1,128)S(1)} %copy.2847), channel_id=39, replica_groups=mesh['gy'=4,'gx'=8] {'gx'}, dimensions={2}, use_global_device_ids=true | all-gather | bytes 4608 | tf_op jit(solution)/shard_map/all_gather | solution.py:62
  1342.0 30.7 %all-gather.36 = f32[2,1,512]{0,1,2:T(1,128)S(1)} all-gather(f32[2,1,64]{0,1,2:T(1,128)S(1)} %copy.2844), channel_id=38, replica_groups=mesh['gy'=4,'gx'=8] {'gx'}, dimensions={2}, use_global_device_ids=true | all-gather | bytes 4608 | tf_op jit(solution)/shard_map/all_gather | solution.py:61
  1375.7 30.8 %all_gather.185 = f32[2,8,256]{1,0,2:T(2,128)S(1)} all-gather(f32[2,8,32]{1,0,2:T(2,128)S(1)} %copy.2850), channel_id=1, replica_groups=mesh['gy'=4,'gx'=8] {'gx'}, dimensions={2}, use_global_device_ids=true | all-gather | bytes 18432 | tf_op jit(solution)/shard_map/all_gather | solution.py:82
  1427.8 30.8 %all-gather.39 = f32[2,1,512]{0,1,2:T(1,128)S(1)} all-gather(f32[2,1,64]{0,1,2:T(1,128)S(1)} %copy.2873), channel_id=41, replica_groups=mesh['gy'=4,'gx'=8] {'gx'}, dimensions={2}, use_global_device_ids=true | all-gather | bytes 4608 | tf_op jit(solution)/shard_map/all_gather | solution.py:62
  1459.3 31.0 %all-gather.38 = f32[2,1,512]{0,1,2:T(1,128)S(1)} all-gather(f32[2,1,64]{0,1,2:T(1,128)S(1)} %copy.2870), channel_id=40, replica_groups=mesh['gy'=4,'gx'=8] {'gx'}, dimensions={2}, use_global_device_ids=true | all-gather | bytes 4608 | tf_op jit(solution)/shard_map/all_gather | solution.py:61
  1492.8 21.0 %all-gather.40 = f32[2,1,1024]{2,1,0:T(1,128)S(1)} all-gather(f32[2,1,128]{2,1,0:T(1,128)S(1)} %get-tuple-element.36), channel_id=42, replica_groups=mesh['gy'=4,'gx'=8] {'gx'}, dimensions={2}, use_global_device_ids=true | all-gather | bytes 9216 | tf_op jit(solution)/shard_map/all_gather | solution.py:61
  1513.8 16.3 all-gather.41
  1540.5 41.9 %psum.62 = f32[]{:T(128)} all-reduce(f32[]{:T(128)} %get-tuple-element.16), channel_id=1, replica_groups=mesh['gy'=4,'gx'=8] {'gy','gx'}, use_global_device_ids=true, to_apply=%region_21.25 | all-reduce | flops 1 | bytes 8 | tf_op jit(solution)/shard_map/psum | solution.py:112
  1598.6 16.6 all-gather.43
  1625.2 41.9 %psum.63 = f32[]{:T(128)} all-reduce(f32[]{:T(128)} %fusion.14), channel_id=1, replica_groups=mesh['gy'=4,'gx'=8] {'gy','gx'}, use_global_device_ids=true, to_apply=%region_23.27 | all-reduce | flops 1 | bytes 8 | tf_op jit(solution)/shard_map/psum | solution.py:112
  (801 shorter events, 369.9 us)
Async XLA Ops:
  0.9 81.3 %collective-permute-start = (f32[2,32,1]{2,1,0:T(8,128)S(1)}, f32[2,32,1]{2,1,0:T(8,128)S(1)}, u32[]{:S(2)}, u32[]{:S(2)}) collective-permute-start(f32[2,32,1]{2,1,0:T(8,128)S(1)} %get-tuple-element.108), channel_id=1, source_target_pairs={{1,0},{2,1},{3,2},{4,3},{5,4},{6,5},{7,6},{0,7},{9,8},{10,9},{11,1... | collective-permute-start | bytes 776 | tf_op jit(solution)/shard_map/ppermute | solution.py:26
  2.3 80.0 %collective-permute-start.1 = (f32[2,32,1]{2,1,0:T(8,128)S(1)}, f32[2,32,1]{2,1,0:T(8,128)S(1)}, u32[]{:S(2)}, u32[]{:S(2)}) collective-permute-start(f32[2,32,1]{2,1,0:T(8,128)S(1)} %get-tuple-element.109), channel_id=1, source_target_pairs={{0,1},{1,2},{2,3},{3,4},{4,5},{5,6},{6,7},{7,0},{8,9},{9,10},{10,1... | collective-permute-start | bytes 776 | tf_op jit(solution)/shard_map/ppermute | solution.py:24
  38.1 44.2 %collective-permute-start.3 = (f32[2,1,128]{2,1,0:T(1,128)S(1)}, f32[2,1,128]{2,1,0:T(1,128)S(1)}, u32[]{:S(2)}, u32[]{:S(2)}) collective-permute-start(f32[2,1,128]{2,1,0:T(1,128)S(1)} %bitcast.402), channel_id=1, source_target_pairs={{0,8},{8,16},{16,24},{24,0},{1,9},{9,17},{17,25},{25,1},{2,10},{10... | collective-permute-start | bytes 3080 | tf_op jit(solution)/shard_map/ppermute | solution.py:24
  70.4 11.9 collective-permute-start.2
  120.4 8.4 collective-permute-start.6
  125.1 4.8 collective-permute-start.7
  133.0 65.1 %collective-permute-start.10 = (f32[2,16,1]{2,1,0:T(8,128)S(1)}, f32[2,16,1]{2,1,0:T(8,128)S(1)}, u32[]{:S(2)}, u32[]{:S(2)}) collective-permute-start(f32[2,16,1]{2,1,0:T(8,128)S(1)} %get-tuple-element.256), channel_id=1, source_target_pairs={{1,0},{2,1},{3,2},{4,3},{5,4},{6,5},{7,6},{0,7},{9,8},{10,9},{11,1... | collective-permute-start | bytes 392 | tf_op jit(solution)/shard_map/ppermute | solution.py:26
  135.9 62.1 %collective-permute-start.11 = (f32[2,16,1]{2,1,0:T(8,128)S(1)}, f32[2,16,1]{2,1,0:T(8,128)S(1)}, u32[]{:S(2)}, u32[]{:S(2)}) collective-permute-start(f32[2,16,1]{2,1,0:T(8,128)S(1)} %get-tuple-element.257), channel_id=1, source_target_pairs={{0,1},{1,2},{2,3},{3,4},{4,5},{5,6},{6,7},{7,0},{8,9},{9,10},{10,1... | collective-permute-start | bytes 392 | tf_op jit(solution)/shard_map/ppermute | solution.py:24
  166.5 31.6 %collective-permute-start.9 = (f32[2,1,64]{2,1,0:T(1,128)S(1)}, f32[2,1,64]{2,1,0:T(1,128)S(1)}, u32[]{:S(2)}, u32[]{:S(2)}) collective-permute-start(f32[2,1,64]{2,1,0:T(1,128)S(1)} %copy.2707), channel_id=1, source_target_pairs={{0,8},{8,16},{16,24},{24,0},{1,9},{9,17},{17,25},{25,1},{2,10},{10... | collective-permute-start | bytes 1544 | tf_op jit(solution)/shard_map/ppermute | solution.py:24
  247.6 67.9 %collective-permute-start.20 = (f32[2,16,1]{2,1,0:T(8,128)S(1)}, f32[2,16,1]{2,1,0:T(8,128)S(1)}, u32[]{:S(2)}, u32[]{:S(2)}) collective-permute-start(f32[2,16,1]{2,1,0:T(8,128)S(1)} %get-tuple-element.226), channel_id=1, source_target_pairs={{1,0},{2,1},{3,2},{4,3},{5,4},{6,5},{7,6},{0,7},{9,8},{10,9},{11,1... | collective-permute-start | bytes 392 | tf_op jit(solution)/shard_map/ppermute | solution.py:26
  252.2 63.3 %collective-permute-start.21 = (f32[2,16,1]{2,1,0:T(8,128)S(1)}, f32[2,16,1]{2,1,0:T(8,128)S(1)}, u32[]{:S(2)}, u32[]{:S(2)}) collective-permute-start(f32[2,16,1]{2,1,0:T(8,128)S(1)} %get-tuple-element.227), channel_id=1, source_target_pairs={{0,1},{1,2},{2,3},{3,4},{4,5},{5,6},{6,7},{7,0},{8,9},{9,10},{10,1... | collective-permute-start | bytes 392 | tf_op jit(solution)/shard_map/ppermute | solution.py:24
  283.9 31.7 %collective-permute-start.19 = (f32[2,1,64]{2,1,0:T(1,128)S(1)}, f32[2,1,64]{2,1,0:T(1,128)S(1)}, u32[]{:S(2)}, u32[]{:S(2)}) collective-permute-start(f32[2,1,64]{2,1,0:T(1,128)S(1)} %copy.2733), channel_id=1, source_target_pairs={{0,8},{8,16},{16,24},{24,0},{1,9},{9,17},{17,25},{25,1},{2,10},{10... | collective-permute-start | bytes 1544 | tf_op jit(solution)/shard_map/ppermute | solution.py:24
  354.2 8.4 collective-permute-start.24
  358.9 4.8 collective-permute-start.25
  398.7 8.9 collective-permute-start.28
  403.4 4.8 collective-permute-start.29
  484.3 8.2 collective-permute-start.32
  488.8 4.8 collective-permute-start.33
  496.6 65.0 %collective-permute-start.36 = (f32[2,16,1]{2,1,0:T(8,128)S(1)}, f32[2,16,1]{2,1,0:T(8,128)S(1)}, u32[]{:S(2)}, u32[]{:S(2)}) collective-permute-start(f32[2,16,1]{2,1,0:T(8,128)S(1)} %get-tuple-element.220), channel_id=1, source_target_pairs={{1,0},{2,1},{3,2},{4,3},{5,4},{6,5},{7,6},{0,7},{9,8},{10,9},{11,1... | collective-permute-start | bytes 392 | tf_op jit(solution)/shard_map/ppermute | solution.py:26
  499.5 62.1 %collective-permute-start.37 = (f32[2,16,1]{2,1,0:T(8,128)S(1)}, f32[2,16,1]{2,1,0:T(8,128)S(1)}, u32[]{:S(2)}, u32[]{:S(2)}) collective-permute-start(f32[2,16,1]{2,1,0:T(8,128)S(1)} %get-tuple-element.221), channel_id=1, source_target_pairs={{0,1},{1,2},{2,3},{3,4},{4,5},{5,6},{6,7},{7,0},{8,9},{9,10},{10,1... | collective-permute-start | bytes 392 | tf_op jit(solution)/shard_map/ppermute | solution.py:24
  530.1 31.5 %collective-permute-start.35 = (f32[2,1,64]{2,1,0:T(1,128)S(1)}, f32[2,1,64]{2,1,0:T(1,128)S(1)}, u32[]{:S(2)}, u32[]{:S(2)}) collective-permute-start(f32[2,1,64]{2,1,0:T(1,128)S(1)} %copy.2753), channel_id=1, source_target_pairs={{0,8},{8,16},{16,24},{24,0},{1,9},{9,17},{17,25},{25,1},{2,10},{10... | collective-permute-start | bytes 1544 | tf_op jit(solution)/shard_map/ppermute | solution.py:24
  611.1 68.2 %collective-permute-start.46 = (f32[2,16,1]{2,1,0:T(8,128)S(1)}, f32[2,16,1]{2,1,0:T(8,128)S(1)}, u32[]{:S(2)}, u32[]{:S(2)}) collective-permute-start(f32[2,16,1]{2,1,0:T(8,128)S(1)} %get-tuple-element.190), channel_id=1, source_target_pairs={{1,0},{2,1},{3,2},{4,3},{5,4},{6,5},{7,6},{0,7},{9,8},{10,9},{11,1... | collective-permute-start | bytes 392 | tf_op jit(solution)/shard_map/ppermute | solution.py:26
  616.1 63.3 %collective-permute-start.47 = (f32[2,16,1]{2,1,0:T(8,128)S(1)}, f32[2,16,1]{2,1,0:T(8,128)S(1)}, u32[]{:S(2)}, u32[]{:S(2)}) collective-permute-start(f32[2,16,1]{2,1,0:T(8,128)S(1)} %get-tuple-element.191), channel_id=1, source_target_pairs={{0,1},{1,2},{2,3},{3,4},{4,5},{5,6},{6,7},{7,0},{8,9},{9,10},{10,1... | collective-permute-start | bytes 392 | tf_op jit(solution)/shard_map/ppermute | solution.py:24
  647.8 31.7 %collective-permute-start.45 = (f32[2,1,64]{2,1,0:T(1,128)S(1)}, f32[2,1,64]{2,1,0:T(1,128)S(1)}, u32[]{:S(2)}, u32[]{:S(2)}) collective-permute-start(f32[2,1,64]{2,1,0:T(1,128)S(1)} %copy.2779), channel_id=1, source_target_pairs={{0,8},{8,16},{16,24},{24,0},{1,9},{9,17},{17,25},{25,1},{2,10},{10... | collective-permute-start | bytes 1544 | tf_op jit(solution)/shard_map/ppermute | solution.py:24
  718.1 8.4 collective-permute-start.50
  722.8 4.8 collective-permute-start.51
  803.2 8.1 collective-permute-start.54
  807.6 4.8 collective-permute-start.55
  888.1 8.4 collective-permute-start.56
  932.5 8.4 collective-permute-start.62
  937.2 4.8 collective-permute-start.63
  945.1 65.0 %collective-permute-start.66 = (f32[2,16,1]{2,1,0:T(8,128)S(1)}, f32[2,16,1]{2,1,0:T(8,128)S(1)}, u32[]{:S(2)}, u32[]{:S(2)}) collective-permute-start(f32[2,16,1]{2,1,0:T(8,128)S(1)} %get-tuple-element.184), channel_id=1, source_target_pairs={{1,0},{2,1},{3,2},{4,3},{5,4},{6,5},{7,6},{0,7},{9,8},{10,9},{11,1... | collective-permute-start | bytes 392 | tf_op jit(solution)/shard_map/ppermute | solution.py:26
  948.0 62.1 %collective-permute-start.67 = (f32[2,16,1]{2,1,0:T(8,128)S(1)}, f32[2,16,1]{2,1,0:T(8,128)S(1)}, u32[]{:S(2)}, u32[]{:S(2)}) collective-permute-start(f32[2,16,1]{2,1,0:T(8,128)S(1)} %get-tuple-element.185), channel_id=1, source_target_pairs={{0,1},{1,2},{2,3},{3,4},{4,5},{5,6},{6,7},{7,0},{8,9},{9,10},{10,1... | collective-permute-start | bytes 392 | tf_op jit(solution)/shard_map/ppermute | solution.py:24
  978.6 31.6 %collective-permute-start.65 = (f32[2,1,64]{2,1,0:T(1,128)S(1)}, f32[2,1,64]{2,1,0:T(1,128)S(1)}, u32[]{:S(2)}, u32[]{:S(2)}) collective-permute-start(f32[2,1,64]{2,1,0:T(1,128)S(1)} %copy.2803), channel_id=1, source_target_pairs={{0,8},{8,16},{16,24},{24,0},{1,9},{9,17},{17,25},{25,1},{2,10},{10... | collective-permute-start | bytes 1544 | tf_op jit(solution)/shard_map/ppermute | solution.py:24
  1059.7 67.9 %collective-permute-start.76 = (f32[2,16,1]{2,1,0:T(8,128)S(1)}, f32[2,16,1]{2,1,0:T(8,128)S(1)}, u32[]{:S(2)}, u32[]{:S(2)}) collective-permute-start(f32[2,16,1]{2,1,0:T(8,128)S(1)} %get-tuple-element.154), channel_id=1, source_target_pairs={{1,0},{2,1},{3,2},{4,3},{5,4},{6,5},{7,6},{0,7},{9,8},{10,9},{11,1... | collective-permute-start | bytes 392 | tf_op jit(solution)/shard_map/ppermute | solution.py:26
  1064.4 63.3 %collective-permute-start.77 = (f32[2,16,1]{2,1,0:T(8,128)S(1)}, f32[2,16,1]{2,1,0:T(8,128)S(1)}, u32[]{:S(2)}, u32[]{:S(2)}) collective-permute-start(f32[2,16,1]{2,1,0:T(8,128)S(1)} %get-tuple-element.155), channel_id=1, source_target_pairs={{0,1},{1,2},{2,3},{3,4},{4,5},{5,6},{6,7},{7,0},{8,9},{9,10},{10,1... | collective-permute-start | bytes 392 | tf_op jit(solution)/shard_map/ppermute | solution.py:24
  1096.0 31.6 %collective-permute-start.75 = (f32[2,1,64]{2,1,0:T(1,128)S(1)}, f32[2,1,64]{2,1,0:T(1,128)S(1)}, u32[]{:S(2)}, u32[]{:S(2)}) collective-permute-start(f32[2,1,64]{2,1,0:T(1,128)S(1)} %copy.2829), channel_id=1, source_target_pairs={{0,8},{8,16},{16,24},{24,0},{1,9},{9,17},{17,25},{25,1},{2,10},{10... | collective-permute-start | bytes 1544 | tf_op jit(solution)/shard_map/ppermute | solution.py:24
  1166.4 8.4 collective-permute-start.80
  1210.8 8.4 collective-permute-start.84
  1296.2 8.1 collective-permute-start.88
  1308.4 65.1 %collective-permute-start.92 = (f32[2,16,1]{2,1,0:T(8,128)S(1)}, f32[2,16,1]{2,1,0:T(8,128)S(1)}, u32[]{:S(2)}, u32[]{:S(2)}) collective-permute-start(f32[2,16,1]{2,1,0:T(8,128)S(1)} %get-tuple-element.148), channel_id=1, source_target_pairs={{1,0},{2,1},{3,2},{4,3},{5,4},{6,5},{7,6},{0,7},{9,8},{10,9},{11,1... | collective-permute-start | bytes 392 | tf_op jit(solution)/shard_map/ppermute | solution.py:26
  1311.4 62.2 %collective-permute-start.93 = (f32[2,16,1]{2,1,0:T(8,128)S(1)}, f32[2,16,1]{2,1,0:T(8,128)S(1)}, u32[]{:S(2)}, u32[]{:S(2)}) collective-permute-start(f32[2,16,1]{2,1,0:T(8,128)S(1)} %get-tuple-element.149), channel_id=1, source_target_pairs={{0,1},{1,2},{2,3},{3,4},{4,5},{5,6},{6,7},{7,0},{8,9},{9,10},{10,1... | collective-permute-start | bytes 392 | tf_op jit(solution)/shard_map/ppermute | solution.py:24
  1342.0 31.5 %collective-permute-start.91 = (f32[2,1,64]{2,1,0:T(1,128)S(1)}, f32[2,1,64]{2,1,0:T(1,128)S(1)}, u32[]{:S(2)}, u32[]{:S(2)}) collective-permute-start(f32[2,1,64]{2,1,0:T(1,128)S(1)} %copy.2849), channel_id=1, source_target_pairs={{0,8},{8,16},{16,24},{24,0},{1,9},{9,17},{17,25},{25,1},{2,10},{10... | collective-permute-start | bytes 1544 | tf_op jit(solution)/shard_map/ppermute | solution.py:24
  1423.0 68.1 %collective-permute-start.102 = (f32[2,16,1]{2,1,0:T(8,128)S(1)}, f32[2,16,1]{2,1,0:T(8,128)S(1)}, u32[]{:S(2)}, u32[]{:S(2)}) collective-permute-start(f32[2,16,1]{2,1,0:T(8,128)S(1)} %get-tuple-element.118), channel_id=1, source_target_pairs={{1,0},{2,1},{3,2},{4,3},{5,4},{6,5},{7,6},{0,7},{9,8},{10,9},{11,1... | collective-permute-start | bytes 392 | tf_op jit(solution)/shard_map/ppermute | solution.py:26
  1427.8 63.3 %collective-permute-start.103 = (f32[2,16,1]{2,1,0:T(8,128)S(1)}, f32[2,16,1]{2,1,0:T(8,128)S(1)}, u32[]{:S(2)}, u32[]{:S(2)}) collective-permute-start(f32[2,16,1]{2,1,0:T(8,128)S(1)} %get-tuple-element.119), channel_id=1, source_target_pairs={{0,1},{1,2},{2,3},{3,4},{4,5},{5,6},{6,7},{7,0},{8,9},{9,10},{10,1... | collective-permute-start | bytes 392 | tf_op jit(solution)/shard_map/ppermute | solution.py:24
  1459.3 31.8 %collective-permute-start.101 = (f32[2,1,64]{2,1,0:T(1,128)S(1)}, f32[2,1,64]{2,1,0:T(1,128)S(1)}, u32[]{:S(2)}, u32[]{:S(2)}) collective-permute-start(f32[2,1,64]{2,1,0:T(1,128)S(1)} %copy.2875), channel_id=1, source_target_pairs={{0,8},{8,16},{16,24},{24,0},{1,9},{9,17},{17,25},{25,1},{2,10},{10... | collective-permute-start | bytes 1544 | tf_op jit(solution)/shard_map/ppermute | solution.py:24
  1530.1 8.4 collective-permute-start.106
  1615.1 8.1 collective-permute-start.110
  (66 other events, 537.5 us)
where the time goes:
time: 1680 us; the launch traced here: 1670 us
  blocking collectives  1370 us (82%)
  starting transfers between devices  124 us (7%)
  local copies, waits for them, and re-layouts  83.3 us (5%)
  waiting for transfers between devices  56.8 us (3%)
    all_gather x22, blocking collectives, operate(): lax.all_gather(field[:, 0, :], 'gx', axis=1, tiled=True)  510 us
    all_gather x22, blocking collectives, operate(): lax.all_gather(field[:, -1, :], 'gx', axis=1, tiled=True)  487 us
    psum x6, blocking collectives, total_inner(): return lax.psum(jnp.sum(first_field * second_field), ('gy', 'gx'))  252 us
    all_gather x4, blocking collectives, coarsest(): gathered = lax.all_gather(residual, 'gx', axis=2, tiled=True)  123 us
    ppermute x56, starting transfers between devices, padded(): lax.ppermute(head, axis, [((i + 1) % count, i) for i in range(count)])  116 us
    ppermute x56, waiting for transfers between devices, padded(): lax.ppermute(tail, axis, [(i, (i + 1) % count) for i in range(count)])  43.9 us
  transfers between devices with their start and end apart: 112, of which 46 were waited for; matrix products, arithmetic and copies ran while one was open for 4% of the time, Pallas kernels for 0%

commit v1 on v0

--- a/solution.py
+++ b/solution.py
@@ -12,6 +12,27 @@
 VERTICAL = 1.0
 REACTION = 0.5
 ADVECTION = 0.5
+
+
+def gather_around(x, axis, dim):
+    peers, position, span = (lax.axis_size(axis), lax.axis_index(axis), x.shape[dim])
+    upward = [(i, (i + 1) % peers) for i in range(peers)]
+    downward = [(i, (i - 1) % peers) for i in range(peers)]
+    filled = jnp.zeros((*x.shape[:dim], peers * span, *x.shape[dim + 1 :]), x.dtype)
+    filled = lax.dynamic_update_slice_in_dim(filled, x, position * span, axis=dim)
+    from_left = from_right = x
+    half = peers // 2
+    for lap in range(1, half + 1):
+        from_left = lax.ppermute(from_left, axis, upward)
+        filled = lax.dynamic_update_slice_in_dim(
+            filled, from_left, (position - lap) % peers * span, axis=dim
+        )
+        if lap < peers - half:
+            from_right = lax.ppermute(from_right, axis, downward)
+            filled = lax.dynamic_update_slice_in_dim(
+                filled, from_right, (position + lap) % peers * span, axis=dim
+            )
+    return filled
 
 
 def padded(cells, sides, width):
@@ -58,7 +79,7 @@
     columns = field.shape[2]
     margins = padded(field, (("gx", 2),), 1)
     bottom_full, upper_full = (
-        lax.all_gather(field[:, 0, :], "gx", axis=1, tiled=True),
+        gather_around(field[:, 0, :], "gx", 1),
         lax.all_gather(field[:, -1, :], "gx", axis=1, tiled=True),
     )
     right_field = margins[:, :, 2:]

time: 1680 us -> 1620 us (0.964)
  blocking collectives: 1370 us -> 954 us
  waiting for transfers between devices: 56.8 us -> 235 us
  starting transfers between devices: 124 us -> 296 us
    all_gather x22 -> x0, blocking collectives: 510 us -> none  [operate(): lax.all_gather(field[:, 0, :], 'gx', axis=1, tiled=True)]
    ppermute x0 -> x154, starting transfers between devices: none -> 206 us  [the longest x66 193 us: gather_around(): from_right = lax.ppermute(from_right, axis, downward)]
    ppermute x0 -> x154, waiting for transfers between devices: none -> 178 us  [the longest x88 177 us: gather_around(): from_left = lax.ppermute(from_left, axis, upward)]
    all_gather x22, blocking collectives: 487 us -> 540 us  [operate(): lax.all_gather(field[:, -1, :], 'gx', axis=1, tiled=True)]
    ppermute x56, starting transfers between devices: 116 us -> 66.6 us  [padded(): lax.ppermute(head, axis, [((i + 1) % count, i) for i in range(count)])]
    psum x6, blocking collectives: 252 us -> 272 us  [total_inner(): return lax.psum(jnp.sum(first_field * second_field), ('gy', 'gx'))]
    all_gather x4, blocking collectives: 123 us -> 142 us  [coarsest(): gathered = lax.all_gather(residual, 'gx', axis=2, tiled=True)]
  transfers between devices with their start and end apart: 112 -> 266, of which waited for: 46 -> 104; matrix products, arithmetic and copies ran while one was open for 4% -> 4% of each run, Pallas kernels for 0% -> 0%
where the time goes in v1:
time: 1620 us; the launch traced here: 1610 us
  blocking collectives  954 us (59%)
  starting transfers between devices  296 us (18%)
  waiting for transfers between devices  235 us (15%)
  local copies, waits for them, and re-layouts  94.4 us (6%)
  between operations  19.1 us (1%)
    all_gather x22, blocking collectives, operate(): lax.all_gather(field[:, -1, :], 'gx', axis=1, tiled=True)  540 us
    psum x6, blocking collectives, total_inner(): return lax.psum(jnp.sum(first_field * second_field), ('gy', 'gx'))  272 us
    ppermute x66, starting transfers between devices, gather_around(): from_right = lax.ppermute(from_right, axis, downward)  193 us
    ppermute x88, waiting for transfers between devices, gather_around(): from_left = lax.ppermute(from_left, axis, upward)  177 us
    all_gather x4, blocking collectives, coarsest(): gathered = lax.all_gather(residual, 'gx', axis=2, tiled=True)  142 us
    ppermute x56, starting transfers between devices, padded(): lax.ppermute(head, axis, [((i + 1) % count, i) for i in range(count)])  66.6 us
  transfers between devices with their start and end apart: 266, of which 104 were waited for; matrix products, arithmetic and copies ran while one was open for 4% of the time, Pallas kernels for 0%

profile of v1, /device:TPU:12, one launch (start us, length us, event | category | flops | bytes accessed | tf_op | source)
XLA Modules:
  0.0 1613.9 jit_solution(13143487693438751650)
XLA Ops:
  6.8 30.5 %all-gather = f32[2,1,1024]{0,2,1:T(8,128)S(1)} all-gather(f32[2,1,128]{0,2,1:T(8,128)S(1)} %copy.3694), channel_id=2, replica_groups=mesh['gy'=4,'gx'=8] {'gx'}, dimensions={2}, use_global_device_ids=true | all-gather | bytes 9216 | tf_op jit(solution)/shard_map/all_gather | solution.py:83
  63.9 5.8 collective-permute-done.8
  76.6 20.9 %all-gather.1 = f32[2,1,1024]{2,1,0:T(1,128)S(1)} all-gather(f32[2,1,128]{2,1,0:T(1,128)S(1)} %get-tuple-element.105), channel_id=3, replica_groups=mesh['gy'=4,'gx'=8] {'gx'}, dimensions={2}, use_global_device_ids=true | all-gather | bytes 9216 | tf_op jit(solution)/shard_map/all_gather | solution.py:83
  98.5 4.8 collective-permute-start.20
  125.4 35.3 %all-gather.2 = f32[2,1,512]{0,1,2:T(1,128)S(1)} all-gather(f32[2,1,64]{0,1,2:T(1,128)S(1)} %copy.3345), channel_id=4, replica_groups=mesh['gy'=4,'gx'=8] {'gx'}, dimensions={2}, use_global_device_ids=true | all-gather | bytes 4608 | tf_op jit(solution)/shard_map/all_gather | solution.py:83
  173.3 5.4 collective-permute-done.28
  181.7 35.5 %all_gather.81 = f32[2,8,256]{1,0,2:T(2,128)S(1)} all-gather(f32[2,8,32]{1,0,2:T(2,128)S(1)} %copy.3348), channel_id=1, replica_groups=mesh['gy'=4,'gx'=8] {'gx'}, dimensions={2}, use_global_device_ids=true | all-gather | bytes 18432 | tf_op jit(solution)/shard_map/all_gather | solution.py:103
  236.6 32.6 %all-gather.3 = f32[2,1,512]{0,1,2:T(1,128)S(1)} all-gather(f32[2,1,64]{0,1,2:T(1,128)S(1)} %copy.3373), channel_id=5, replica_groups=mesh['gy'=4,'gx'=8] {'gx'}, dimensions={2}, use_global_device_ids=true | all-gather | bytes 4608 | tf_op jit(solution)/shard_map/all_gather | solution.py:83
  281.9 5.4 collective-permute-done.45
  289.9 4.8 collective-permute-start.51
  294.7 20.9 %all-gather.4 = f32[2,1,1024]{2,1,0:T(1,128)S(1)} all-gather(f32[2,1,128]{2,1,0:T(1,128)S(1)} %get-tuple-element.99), channel_id=6, replica_groups=mesh['gy'=4,'gx'=8] {'gx'}, dimensions={2}, use_global_device_ids=true | all-gather | bytes 9216 | tf_op jit(solution)/shard_map/all_gather | solution.py:83
  316.7 4.8 collective-permute-start.59
  341.1 20.8 %all-gather.5 = f32[2,1,1024]{2,1,0:T(1,128)S(1)} all-gather(f32[2,1,128]{2,1,0:T(1,128)S(1)} %get-tuple-element.91), channel_id=7, replica_groups=mesh['gy'=4,'gx'=8] {'gx'}, dimensions={2}, use_global_device_ids=true | all-gather | bytes 9216 | tf_op jit(solution)/shard_map/all_gather | solution.py:83
  362.8 4.8 collective-permute-start.70
  384.7 45.5 %all-reduce.1 = (f32[]{:T(128)}, f32[]{:T(128)}) all-reduce(f32[]{:T(128)} %get-tuple-element.11, f32[]{:T(128)} %get-tuple-element.10), channel_id=1, replica_groups=mesh['gy'=4,'gx'=8] {'gy','gx'}, use_global_device_ids=true, to_apply=%region_3.7 | all-reduce | flops 2 | bytes 16 | tf_op jit(solution)/shard_map/psum | solution.py:133
  434.7 14.0 all-gather.6
  449.7 4.8 collective-permute-start.81
  476.6 35.2 %all-gather.7 = f32[2,1,512]{0,1,2:T(1,128)S(1)} all-gather(f32[2,1,64]{0,1,2:T(1,128)S(1)} %copy.3416), channel_id=9, replica_groups=mesh['gy'=4,'gx'=8] {'gx'}, dimensions={2}, use_global_device_ids=true | all-gather | bytes 4608 | tf_op jit(solution)/shard_map/all_gather | solution.py:83
  524.7 5.2 collective-permute-done.89
  532.8 35.7 %all_gather.87 = f32[2,8,256]{1,0,2:T(2,128)S(1)} all-gather(f32[2,8,32]{1,0,2:T(2,128)S(1)} %copy.3419), channel_id=1, replica_groups=mesh['gy'=4,'gx'=8] {'gx'}, dimensions={2}, use_global_device_ids=true | all-gather | bytes 18432 | tf_op jit(solution)/shard_map/all_gather | solution.py:103
  588.3 32.6 %all-gather.8 = f32[2,1,512]{0,1,2:T(1,128)S(1)} all-gather(f32[2,1,64]{0,1,2:T(1,128)S(1)} %copy.3444), channel_id=10, replica_groups=mesh['gy'=4,'gx'=8] {'gx'}, dimensions={2}, use_global_device_ids=true | all-gather | bytes 4608 | tf_op jit(solution)/shard_map/all_gather | solution.py:83
  633.7 5.2 collective-permute-done.106
  646.3 20.9 %all-gather.9 = f32[2,1,1024]{2,1,0:T(1,128)S(1)} all-gather(f32[2,1,128]{2,1,0:T(1,128)S(1)} %get-tuple-element.79), channel_id=11, replica_groups=mesh['gy'=4,'gx'=8] {'gx'}, dimensions={2}, use_global_device_ids=true | all-gather | bytes 9216 | tf_op jit(solution)/shard_map/all_gather | solution.py:83
  690.1 45.5 %psum.58 = f32[]{:T(128)} all-reduce(f32[]{:T(128)} %get-tuple-element.23), channel_id=1, replica_groups=mesh['gy'=4,'gx'=8] {'gy','gx'}, use_global_device_ids=true, to_apply=%region_9.13 | all-reduce | flops 1 | bytes 8 | tf_op jit(solution)/shard_map/psum | solution.py:133
  740.0 14.0 all-gather.10
  776.8 45.1 %psum.59 = f32[]{:T(128)} all-reduce(f32[]{:T(128)} %fusion.65), channel_id=1, replica_groups=mesh['gy'=4,'gx'=8] {'gy','gx'}, use_global_device_ids=true, to_apply=%region_11.15 | all-reduce | flops 1 | bytes 8 | tf_op jit(solution)/shard_map/psum | solution.py:133
  826.5 14.3 all-gather.11
  865.9 20.9 %all-gather.12 = f32[2,1,1024]{2,1,0:T(1,128)S(1)} all-gather(f32[2,1,128]{2,1,0:T(1,128)S(1)} %get-tuple-element.63), channel_id=14, replica_groups=mesh['gy'=4,'gx'=8] {'gx'}, dimensions={2}, use_global_device_ids=true | all-gather | bytes 9216 | tf_op jit(solution)/shard_map/all_gather | solution.py:83
  887.8 4.9 collective-permute-start.153
  914.9 35.2 %all-gather.13 = f32[2,1,512]{0,1,2:T(1,128)S(1)} all-gather(f32[2,1,64]{0,1,2:T(1,128)S(1)} %copy.3498), channel_id=15, replica_groups=mesh['gy'=4,'gx'=8] {'gx'}, dimensions={2}, use_global_device_ids=true | all-gather | bytes 4608 | tf_op jit(solution)/shard_map/all_gather | solution.py:83
  962.8 5.3 collective-permute-done.161
  971.1 35.5 %all_gather.94 = f32[2,8,256]{1,0,2:T(2,128)S(1)} all-gather(f32[2,8,32]{1,0,2:T(2,128)S(1)} %copy.3501), channel_id=1, replica_groups=mesh['gy'=4,'gx'=8] {'gx'}, dimensions={2}, use_global_device_ids=true | all-gather | bytes 18432 | tf_op jit(solution)/shard_map/all_gather | solution.py:103
  1026.0 32.6 %all-gather.14 = f32[2,1,512]{0,1,2:T(1,128)S(1)} all-gather(f32[2,1,64]{0,1,2:T(1,128)S(1)} %copy.3526), channel_id=16, replica_groups=mesh['gy'=4,'gx'=8] {'gx'}, dimensions={2}, use_global_device_ids=true | all-gather | bytes 4608 | tf_op jit(solution)/shard_map/all_gather | solution.py:83
  1071.4 5.2 collective-permute-done.178
  1084.0 20.9 %all-gather.15 = f32[2,1,1024]{2,1,0:T(1,128)S(1)} all-gather(f32[2,1,128]{2,1,0:T(1,128)S(1)} %get-tuple-element.57), channel_id=17, replica_groups=mesh['gy'=4,'gx'=8] {'gx'}, dimensions={2}, use_global_device_ids=true | all-gather | bytes 9216 | tf_op jit(solution)/shard_map/all_gather | solution.py:83
  1130.4 20.8 %all-gather.16 = f32[2,1,1024]{2,1,0:T(1,128)S(1)} all-gather(f32[2,1,128]{2,1,0:T(1,128)S(1)} %get-tuple-element.49), channel_id=18, replica_groups=mesh['gy'=4,'gx'=8] {'gx'}, dimensions={2}, use_global_device_ids=true | all-gather | bytes 9216 | tf_op jit(solution)/shard_map/all_gather | solution.py:83
  1152.2 5.0 collective-permute-start.203
  1174.5 45.3 %all-reduce = (f32[]{:T(128)}, f32[]{:T(128)}) all-reduce(f32[]{:T(128)} %get-tuple-element.8, f32[]{:T(128)} %get-tuple-element.6), channel_id=1, replica_groups=mesh['gy'=4,'gx'=8] {'gy','gx'}, use_global_device_ids=true, to_apply=%region_15.19 | all-reduce | flops 2 | bytes 16 | tf_op jit(solution)/shard_map/psum | solution.py:133
  1224.3 14.1 all-gather.17
  1266.2 35.4 %all-gather.18 = f32[2,1,512]{0,1,2:T(1,128)S(1)} all-gather(f32[2,1,64]{0,1,2:T(1,128)S(1)} %copy.3569), channel_id=20, replica_groups=mesh['gy'=4,'gx'=8] {'gx'}, dimensions={2}, use_global_device_ids=true | all-gather | bytes 4608 | tf_op jit(solution)/shard_map/all_gather | solution.py:83
  1314.3 5.2 collective-permute-done.222
  1322.5 35.7 %all_gather.100 = f32[2,8,256]{1,0,2:T(2,128)S(1)} all-gather(f32[2,8,32]{1,0,2:T(2,128)S(1)} %copy.3572), channel_id=1, replica_groups=mesh['gy'=4,'gx'=8] {'gx'}, dimensions={2}, use_global_device_ids=true | all-gather | bytes 18432 | tf_op jit(solution)/shard_map/all_gather | solution.py:103
  1377.6 32.6 %all-gather.19 = f32[2,1,512]{0,1,2:T(1,128)S(1)} all-gather(f32[2,1,64]{0,1,2:T(1,128)S(1)} %copy.3597), channel_id=21, replica_groups=mesh['gy'=4,'gx'=8] {'gx'}, dimensions={2}, use_global_device_ids=true | all-gather | bytes 4608 | tf_op jit(solution)/shard_map/all_gather | solution.py:83
  1423.0 5.2 collective-permute-done.239
  1435.8 20.9 %all-gather.20 = f32[2,1,1024]{2,1,0:T(1,128)S(1)} all-gather(f32[2,1,128]{2,1,0:T(1,128)S(1)} %get-tuple-element.37), channel_id=22, replica_groups=mesh['gy'=4,'gx'=8] {'gx'}, dimensions={2}, use_global_device_ids=true | all-gather | bytes 9216 | tf_op jit(solution)/shard_map/all_gather | solution.py:83
  1479.6 45.5 %psum.62 = f32[]{:T(128)} all-reduce(f32[]{:T(128)} %get-tuple-element.16), channel_id=1, replica_groups=mesh['gy'=4,'gx'=8] {'gy','gx'}, use_global_device_ids=true, to_apply=%region_21.25 | all-reduce | flops 1 | bytes 8 | tf_op jit(solution)/shard_map/psum | solution.py:133
  1529.5 14.0 all-gather.21
  1566.3 45.1 %psum.63 = f32[]{:T(128)} all-reduce(f32[]{:T(128)} %fusion.14), channel_id=1, replica_groups=mesh['gy'=4,'gx'=8] {'gy','gx'}, use_global_device_ids=true, to_apply=%region_23.27 | all-reduce | flops 1 | bytes 8 | tf_op jit(solution)/shard_map/psum | solution.py:133
  (1376 shorter events, 559.1 us)
Async XLA Ops:
  0.9 52.3 %collective-permute-start.2 = (f32[2,128]{0,1:T(8,128)S(1)}, f32[2,128]{0,1:T(8,128)S(1)}, u32[]{:S(2)}, u32[]{:S(2)}) collective-permute-start(f32[2,128]{0,1:T(8,128)S(1)} %bitcast.349), channel_id=1, source_target_pairs={{0,1},{1,2},{2,3},{3,4},{4,5},{5,6},{6,7},{7,0},{8,9},{9,10},{10,1... | collective-permute-start | bytes 3080 | tf_op jit(solution)/shard_map/ppermute | solution.py:26
  2.4 50.9 %collective-permute-start.3 = (f32[2,128]{0,1:T(8,128)S(1)}, f32[2,128]{0,1:T(8,128)S(1)}, u32[]{:S(2)}, u32[]{:S(2)}) collective-permute-start(f32[2,128]{0,1:T(8,128)S(1)} %bitcast.350), channel_id=1, source_target_pairs={{0,7},{1,0},{2,1},{3,2},{4,3},{5,4},{6,5},{7,6},{8,15},{9,8},{10,9... | collective-permute-start | bytes 3080 | tf_op jit(solution)/shard_map/ppermute | solution.py:31
  38.0 33.0 %collective-permute-start.10 = (f32[2,1,128]{2,1,0:T(1,128)S(1)}, f32[2,1,128]{2,1,0:T(1,128)S(1)}, u32[]{:S(2)}, u32[]{:S(2)}) collective-permute-start(f32[2,1,128]{2,1,0:T(1,128)S(1)} %bitcast.430), channel_id=1, source_target_pairs={{0,8},{8,16},{16,24},{24,0},{1,9},{9,17},{17,25},{25,1},{2,10},{10... | collective-permute-start | bytes 3080 | tf_op jit(solution)/shard_map/ppermute | solution.py:45
  38.9 32.0 %collective-permute-start = (f32[2,32,1]{2,1,0:T(8,128)S(1)}, f32[2,32,1]{2,1,0:T(8,128)S(1)}, u32[]{:S(2)}, u32[]{:S(2)}) collective-permute-start(f32[2,32,1]{2,1,0:T(8,128)S(1)} %get-tuple-element.108), channel_id=1, source_target_pairs={{1,0},{2,1},{3,2},{4,3},{5,4},{6,5},{7,6},{0,7},{9,8},{10,9},{11,1... | collective-permute-start | bytes 776 | tf_op jit(solution)/shard_map/ppermute | solution.py:47
  40.6 30.4 %collective-permute-start.1 = (f32[2,32,1]{2,1,0:T(8,128)S(1)}, f32[2,32,1]{2,1,0:T(8,128)S(1)}, u32[]{:S(2)}, u32[]{:S(2)}) collective-permute-start(f32[2,32,1]{2,1,0:T(8,128)S(1)} %get-tuple-element.109), channel_id=1, source_target_pairs={{0,1},{1,2},{2,3},{3,4},{4,5},{5,6},{6,7},{7,0},{8,9},{9,10},{10,1... | collective-permute-start | bytes 776 | tf_op jit(solution)/shard_map/ppermute | solution.py:45
  72.5 30.9 %collective-permute-start.11 = (f32[2,128]{1,0:T(2,128)S(1)}, f32[2,128]{1,0:T(2,128)S(1)}, u32[]{:S(2)}, u32[]{:S(2)}) collective-permute-start(f32[2,128]{1,0:T(2,128)S(1)} %bitcast.390), channel_id=1, source_target_pairs={{0,1},{1,2},{2,3},{3,4},{4,5},{5,6},{6,7},{7,0},{8,9},{9,10},{10,1... | collective-permute-start | bytes 3080 | tf_op jit(solution)/shard_map/ppermute | solution.py:26
  72.5 31.2 %collective-permute-start.12 = (f32[2,128]{1,0:T(2,128)S(1)}, f32[2,128]{1,0:T(2,128)S(1)}, u32[]{:S(2)}, u32[]{:S(2)}) collective-permute-start(f32[2,128]{1,0:T(2,128)S(1)} %bitcast.391), channel_id=1, source_target_pairs={{0,7},{1,0},{2,1},{3,2},{4,3},{5,4},{6,5},{7,6},{8,15},{9,8},{10,9... | collective-permute-start | bytes 3080 | tf_op jit(solution)/shard_map/ppermute | solution.py:31
  122.3 41.3 %collective-permute-start.22 = (f32[2,64]{0,1:T(8,128)S(1)}, f32[2,64]{0,1:T(8,128)S(1)}, u32[]{:S(2)}, u32[]{:S(2)}) collective-permute-start(f32[2,64]{0,1:T(8,128)S(1)} %copy.3340), channel_id=1, source_target_pairs={{0,1},{1,2},{2,3},{3,4},{4,5},{5,6},{6,7},{7,0},{8,9},{9,10},{10,1... | collective-permute-start | bytes 1544 | tf_op jit(solution)/shard_map/ppermute | solution.py:26
  122.3 41.3 %collective-permute-start.23 = (f32[2,64]{0,1:T(8,128)S(1)}, f32[2,64]{0,1:T(8,128)S(1)}, u32[]{:S(2)}, u32[]{:S(2)}) collective-permute-start(f32[2,64]{0,1:T(8,128)S(1)} %copy.3340), channel_id=1, source_target_pairs={{0,7},{1,0},{2,1},{3,2},{4,3},{5,4},{6,5},{7,6},{8,15},{9,8},{10,9... | collective-permute-start | bytes 1544 | tf_op jit(solution)/shard_map/ppermute | solution.py:31
  233.5 38.6 %collective-permute-start.39 = (f32[2,64]{0,1:T(8,128)S(1)}, f32[2,64]{0,1:T(8,128)S(1)}, u32[]{:S(2)}, u32[]{:S(2)}) collective-permute-start(f32[2,64]{0,1:T(8,128)S(1)} %copy.3368), channel_id=1, source_target_pairs={{0,1},{1,2},{2,3},{3,4},{4,5},{5,6},{6,7},{7,0},{8,9},{9,10},{10,1... | collective-permute-start | bytes 1544 | tf_op jit(solution)/shard_map/ppermute | solution.py:26
  233.5 38.8 %collective-permute-start.40 = (f32[2,64]{0,1:T(8,128)S(1)}, f32[2,64]{0,1:T(8,128)S(1)}, u32[]{:S(2)}, u32[]{:S(2)}) collective-permute-start(f32[2,64]{0,1:T(8,128)S(1)} %copy.3368), channel_id=1, source_target_pairs={{0,7},{1,0},{2,1},{3,2},{4,3},{5,4},{6,5},{7,6},{8,15},{9,8},{10,9... | collective-permute-start | bytes 1544 | tf_op jit(solution)/shard_map/ppermute | solution.py:31
  289.8 31.7 %collective-permute-start.50 = (f32[2,128]{1,0:T(2,128)S(1)}, f32[2,128]{1,0:T(2,128)S(1)}, u32[]{:S(2)}, u32[]{:S(2)}) collective-permute-start(f32[2,128]{1,0:T(2,128)S(1)} %bitcast.393), channel_id=1, source_target_pairs={{0,1},{1,2},{2,3},{3,4},{4,5},{5,6},{6,7},{7,0},{8,9},{9,10},{10,1... | collective-permute-start | bytes 3080 | tf_op jit(solution)/shard_map/ppermute | solution.py:26
  289.9 32.0 %collective-permute-start.51 = (f32[2,128]{1,0:T(2,128)S(1)}, f32[2,128]{1,0:T(2,128)S(1)}, u32[]{:S(2)}, u32[]{:S(2)}) collective-permute-start(f32[2,128]{1,0:T(2,128)S(1)} %bitcast.394), channel_id=1, source_target_pairs={{0,7},{1,0},{2,1},{3,2},{4,3},{5,4},{6,5},{7,6},{8,15},{9,8},{10,9... | collective-permute-start | bytes 3080 | tf_op jit(solution)/shard_map/ppermute | solution.py:31
  338.0 29.6 %collective-permute-start.61 = (f32[2,128]{1,0:T(2,128)S(1)}, f32[2,128]{1,0:T(2,128)S(1)}, u32[]{:S(2)}, u32[]{:S(2)}) collective-permute-start(f32[2,128]{1,0:T(2,128)S(1)} %bitcast.396), channel_id=1, source_target_pairs={{0,1},{1,2},{2,3},{3,4},{4,5},{5,6},{6,7},{7,0},{8,9},{9,10},{10,1... | collective-permute-start | bytes 3080 | tf_op jit(solution)/shard_map/ppermute | solution.py:26
  338.1 30.0 %collective-permute-start.62 = (f32[2,128]{1,0:T(2,128)S(1)}, f32[2,128]{1,0:T(2,128)S(1)}, u32[]{:S(2)}, u32[]{:S(2)}) collective-permute-start(f32[2,128]{1,0:T(2,128)S(1)} %bitcast.397), channel_id=1, source_target_pairs={{0,7},{1,0},{2,1},{3,2},{4,3},{5,4},{6,5},{7,6},{8,15},{9,8},{10,9... | collective-permute-start | bytes 3080 | tf_op jit(solution)/shard_map/ppermute | solution.py:31
  431.7 22.9 %collective-permute-start.72 = (f32[2,128]{1,0:T(2,128)S(1)}, f32[2,128]{1,0:T(2,128)S(1)}, u32[]{:S(2)}, u32[]{:S(2)}) collective-permute-start(f32[2,128]{1,0:T(2,128)S(1)} %bitcast.399), channel_id=1, source_target_pairs={{0,1},{1,2},{2,3},{3,4},{4,5},{5,6},{6,7},{7,0},{8,9},{9,10},{10,1... | collective-permute-start | bytes 3080 | tf_op jit(solution)/shard_map/ppermute | solution.py:26
  432.6 22.4 %collective-permute-start.73 = (f32[2,128]{1,0:T(2,128)S(1)}, f32[2,128]{1,0:T(2,128)S(1)}, u32[]{:S(2)}, u32[]{:S(2)}) collective-permute-start(f32[2,128]{1,0:T(2,128)S(1)} %bitcast.400), channel_id=1, source_target_pairs={{0,7},{1,0},{2,1},{3,2},{4,3},{5,4},{6,5},{7,6},{8,15},{9,8},{10,9... | collective-permute-start | bytes 3080 | tf_op jit(solution)/shard_map/ppermute | solution.py:31
  473.5 41.2 %collective-permute-start.83 = (f32[2,64]{0,1:T(8,128)S(1)}, f32[2,64]{0,1:T(8,128)S(1)}, u32[]{:S(2)}, u32[]{:S(2)}) collective-permute-start(f32[2,64]{0,1:T(8,128)S(1)} %copy.3411), channel_id=1, source_target_pairs={{0,1},{1,2},{2,3},{3,4},{4,5},{5,6},{6,7},{7,0},{8,9},{9,10},{10,1... | collective-permute-start | bytes 1544 | tf_op jit(solution)/shard_map/ppermute | solution.py:26
  473.5 41.2 %collective-permute-start.84 = (f32[2,64]{0,1:T(8,128)S(1)}, f32[2,64]{0,1:T(8,128)S(1)}, u32[]{:S(2)}, u32[]{:S(2)}) collective-permute-start(f32[2,64]{0,1:T(8,128)S(1)} %copy.3411), channel_id=1, source_target_pairs={{0,7},{1,0},{2,1},{3,2},{4,3},{5,4},{6,5},{7,6},{8,15},{9,8},{10,9... | collective-permute-start | bytes 1544 | tf_op jit(solution)/shard_map/ppermute | solution.py:31
  585.2 38.6 %collective-permute-start.100 = (f32[2,64]{0,1:T(8,128)S(1)}, f32[2,64]{0,1:T(8,128)S(1)}, u32[]{:S(2)}, u32[]{:S(2)}) collective-permute-start(f32[2,64]{0,1:T(8,128)S(1)} %copy.3439), channel_id=1, source_target_pairs={{0,1},{1,2},{2,3},{3,4},{4,5},{5,6},{6,7},{7,0},{8,9},{9,10},{10,1... | collective-permute-start | bytes 1544 | tf_op jit(solution)/shard_map/ppermute | solution.py:26
  585.2 38.6 %collective-permute-start.101 = (f32[2,64]{0,1:T(8,128)S(1)}, f32[2,64]{0,1:T(8,128)S(1)}, u32[]{:S(2)}, u32[]{:S(2)}) collective-permute-start(f32[2,64]{0,1:T(8,128)S(1)} %copy.3439), channel_id=1, source_target_pairs={{0,7},{1,0},{2,1},{3,2},{4,3},{5,4},{6,5},{7,6},{8,15},{9,8},{10,9... | collective-permute-start | bytes 1544 | tf_op jit(solution)/shard_map/ppermute | solution.py:31
  641.4 31.6 %collective-permute-start.111 = (f32[2,128]{1,0:T(2,128)S(1)}, f32[2,128]{1,0:T(2,128)S(1)}, u32[]{:S(2)}, u32[]{:S(2)}) collective-permute-start(f32[2,128]{1,0:T(2,128)S(1)} %bitcast.402), channel_id=1, source_target_pairs={{0,1},{1,2},{2,3},{3,4},{4,5},{5,6},{6,7},{7,0},{8,9},{9,10},{10,1... | collective-permute-start | bytes 3080 | tf_op jit(solution)/shard_map/ppermute | solution.py:26
  641.5 32.0 %collective-permute-start.112 = (f32[2,128]{1,0:T(2,128)S(1)}, f32[2,128]{1,0:T(2,128)S(1)}, u32[]{:S(2)}, u32[]{:S(2)}) collective-permute-start(f32[2,128]{1,0:T(2,128)S(1)} %bitcast.403), channel_id=1, source_target_pairs={{0,7},{1,0},{2,1},{3,2},{4,3},{5,4},{6,5},{7,6},{8,15},{9,8},{10,9... | collective-permute-start | bytes 3080 | tf_op jit(solution)/shard_map/ppermute | solution.py:31
  736.9 22.8 %collective-permute-start.122 = (f32[2,128]{1,0:T(2,128)S(1)}, f32[2,128]{1,0:T(2,128)S(1)}, u32[]{:S(2)}, u32[]{:S(2)}) collective-permute-start(f32[2,128]{1,0:T(2,128)S(1)} %bitcast.387), channel_id=1, source_target_pairs={{0,1},{1,2},{2,3},{3,4},{4,5},{5,6},{6,7},{7,0},{8,9},{9,10},{10,1... | collective-permute-start | bytes 3080 | tf_op jit(solution)/shard_map/ppermute | solution.py:26
  737.9 22.3 %collective-permute-start.123 = (f32[2,128]{1,0:T(2,128)S(1)}, f32[2,128]{1,0:T(2,128)S(1)}, u32[]{:S(2)}, u32[]{:S(2)}) collective-permute-start(f32[2,128]{1,0:T(2,128)S(1)} %bitcast.388), channel_id=1, source_target_pairs={{0,7},{1,0},{2,1},{3,2},{4,3},{5,4},{6,5},{7,6},{8,15},{9,8},{10,9... | collective-permute-start | bytes 3080 | tf_op jit(solution)/shard_map/ppermute | solution.py:31
  823.5 22.8 %collective-permute-start.135 = (f32[2,128]{1,0:T(2,128)S(1)}, f32[2,128]{1,0:T(2,128)S(1)}, u32[]{:S(2)}, u32[]{:S(2)}) collective-permute-start(f32[2,128]{1,0:T(2,128)S(1)} %bitcast.405), channel_id=1, source_target_pairs={{0,1},{1,2},{2,3},{3,4},{4,5},{5,6},{6,7},{7,0},{8,9},{9,10},{10,1... | collective-permute-start | bytes 3080 | tf_op jit(solution)/shard_map/ppermute | solution.py:26
  824.9 21.9 %collective-permute-start.136 = (f32[2,128]{1,0:T(2,128)S(1)}, f32[2,128]{1,0:T(2,128)S(1)}, u32[]{:S(2)}, u32[]{:S(2)}) collective-permute-start(f32[2,128]{1,0:T(2,128)S(1)} %bitcast.406), channel_id=1, source_target_pairs={{0,7},{1,0},{2,1},{3,2},{4,3},{5,4},{6,5},{7,6},{8,15},{9,8},{10,9... | collective-permute-start | bytes 3080 | tf_op jit(solution)/shard_map/ppermute | solution.py:31
  862.8 30.0 %collective-permute-start.144 = (f32[2,128]{1,0:T(2,128)S(1)}, f32[2,128]{1,0:T(2,128)S(1)}, u32[]{:S(2)}, u32[]{:S(2)}) collective-permute-start(f32[2,128]{1,0:T(2,128)S(1)} %bitcast.408), channel_id=1, source_target_pairs={{0,1},{1,2},{2,3},{3,4},{4,5},{5,6},{6,7},{7,0},{8,9},{9,10},{10,1... | collective-permute-start | bytes 3080 | tf_op jit(solution)/shard_map/ppermute | solution.py:26
  862.9 30.4 %collective-permute-start.145 = (f32[2,128]{1,0:T(2,128)S(1)}, f32[2,128]{1,0:T(2,128)S(1)}, u32[]{:S(2)}, u32[]{:S(2)}) collective-permute-start(f32[2,128]{1,0:T(2,128)S(1)} %bitcast.409), channel_id=1, source_target_pairs={{0,7},{1,0},{2,1},{3,2},{4,3},{5,4},{6,5},{7,6},{8,15},{9,8},{10,9... | collective-permute-start | bytes 3080 | tf_op jit(solution)/shard_map/ppermute | solution.py:31
  911.8 41.2 %collective-permute-start.155 = (f32[2,64]{0,1:T(8,128)S(1)}, f32[2,64]{0,1:T(8,128)S(1)}, u32[]{:S(2)}, u32[]{:S(2)}) collective-permute-start(f32[2,64]{0,1:T(8,128)S(1)} %copy.3493), channel_id=1, source_target_pairs={{0,1},{1,2},{2,3},{3,4},{4,5},{5,6},{6,7},{7,0},{8,9},{9,10},{10,1... | collective-permute-start | bytes 1544 | tf_op jit(solution)/shard_map/ppermute | solution.py:26
  911.8 41.2 %collective-permute-start.156 = (f32[2,64]{0,1:T(8,128)S(1)}, f32[2,64]{0,1:T(8,128)S(1)}, u32[]{:S(2)}, u32[]{:S(2)}) collective-permute-start(f32[2,64]{0,1:T(8,128)S(1)} %copy.3493), channel_id=1, source_target_pairs={{0,7},{1,0},{2,1},{3,2},{4,3},{5,4},{6,5},{7,6},{8,15},{9,8},{10,9... | collective-permute-start | bytes 1544 | tf_op jit(solution)/shard_map/ppermute | solution.py:31
  1022.9 38.6 %collective-permute-start.172 = (f32[2,64]{0,1:T(8,128)S(1)}, f32[2,64]{0,1:T(8,128)S(1)}, u32[]{:S(2)}, u32[]{:S(2)}) collective-permute-start(f32[2,64]{0,1:T(8,128)S(1)} %copy.3521), channel_id=1, source_target_pairs={{0,1},{1,2},{2,3},{3,4},{4,5},{5,6},{6,7},{7,0},{8,9},{9,10},{10,1... | collective-permute-start | bytes 1544 | tf_op jit(solution)/shard_map/ppermute | solution.py:26
  1022.9 38.6 %collective-permute-start.173 = (f32[2,64]{0,1:T(8,128)S(1)}, f32[2,64]{0,1:T(8,128)S(1)}, u32[]{:S(2)}, u32[]{:S(2)}) collective-permute-start(f32[2,64]{0,1:T(8,128)S(1)} %copy.3521), channel_id=1, source_target_pairs={{0,7},{1,0},{2,1},{3,2},{4,3},{5,4},{6,5},{7,6},{8,15},{9,8},{10,9... | collective-permute-start | bytes 1544 | tf_op jit(solution)/shard_map/ppermute | solution.py:31
  1079.1 31.6 %collective-permute-start.183 = (f32[2,128]{1,0:T(2,128)S(1)}, f32[2,128]{1,0:T(2,128)S(1)}, u32[]{:S(2)}, u32[]{:S(2)}) collective-permute-start(f32[2,128]{1,0:T(2,128)S(1)} %bitcast.411), channel_id=1, source_target_pairs={{0,1},{1,2},{2,3},{3,4},{4,5},{5,6},{6,7},{7,0},{8,9},{9,10},{10,1... | collective-permute-start | bytes 3080 | tf_op jit(solution)/shard_map/ppermute | solution.py:26
  1079.2 32.0 %collective-permute-start.184 = (f32[2,128]{1,0:T(2,128)S(1)}, f32[2,128]{1,0:T(2,128)S(1)}, u32[]{:S(2)}, u32[]{:S(2)}) collective-permute-start(f32[2,128]{1,0:T(2,128)S(1)} %bitcast.412), channel_id=1, source_target_pairs={{0,7},{1,0},{2,1},{3,2},{4,3},{5,4},{6,5},{7,6},{8,15},{9,8},{10,9... | collective-permute-start | bytes 3080 | tf_op jit(solution)/shard_map/ppermute | solution.py:31
  1127.3 29.8 %collective-permute-start.194 = (f32[2,128]{1,0:T(2,128)S(1)}, f32[2,128]{1,0:T(2,128)S(1)}, u32[]{:S(2)}, u32[]{:S(2)}) collective-permute-start(f32[2,128]{1,0:T(2,128)S(1)} %bitcast.414), channel_id=1, source_target_pairs={{0,1},{1,2},{2,3},{3,4},{4,5},{5,6},{6,7},{7,0},{8,9},{9,10},{10,1... | collective-permute-start | bytes 3080 | tf_op jit(solution)/shard_map/ppermute | solution.py:26
  1127.4 30.2 %collective-permute-start.195 = (f32[2,128]{1,0:T(2,128)S(1)}, f32[2,128]{1,0:T(2,128)S(1)}, u32[]{:S(2)}, u32[]{:S(2)}) collective-permute-start(f32[2,128]{1,0:T(2,128)S(1)} %bitcast.415), channel_id=1, source_target_pairs={{0,7},{1,0},{2,1},{3,2},{4,3},{5,4},{6,5},{7,6},{8,15},{9,8},{10,9... | collective-permute-start | bytes 3080 | tf_op jit(solution)/shard_map/ppermute | solution.py:31
  1152.1 20.4 %collective-permute-start.202 = (f32[2,1,128]{2,1,0:T(1,128)S(1)}, f32[2,1,128]{2,1,0:T(1,128)S(1)}, u32[]{:S(2)}, u32[]{:S(2)}) collective-permute-start(f32[2,1,128]{2,1,0:T(1,128)S(1)} %bitcast.441), channel_id=1, source_target_pairs={{0,8},{8,16},{16,24},{24,0},{1,9},{9,17},{17,25},{25,1},{2,10},{10... | collective-permute-start | bytes 3080 | tf_op jit(solution)/shard_map/ppermute | solution.py:45
  1221.2 22.9 %collective-permute-start.205 = (f32[2,128]{1,0:T(2,128)S(1)}, f32[2,128]{1,0:T(2,128)S(1)}, u32[]{:S(2)}, u32[]{:S(2)}) collective-permute-start(f32[2,128]{1,0:T(2,128)S(1)} %bitcast.417), channel_id=1, source_target_pairs={{0,1},{1,2},{2,3},{3,4},{4,5},{5,6},{6,7},{7,0},{8,9},{9,10},{10,1... | collective-permute-start | bytes 3080 | tf_op jit(solution)/shard_map/ppermute | solution.py:26
  1222.4 22.1 %collective-permute-start.206 = (f32[2,128]{1,0:T(2,128)S(1)}, f32[2,128]{1,0:T(2,128)S(1)}, u32[]{:S(2)}, u32[]{:S(2)}) collective-permute-start(f32[2,128]{1,0:T(2,128)S(1)} %bitcast.418), channel_id=1, source_target_pairs={{0,7},{1,0},{2,1},{3,2},{4,3},{5,4},{6,5},{7,6},{8,15},{9,8},{10,9... | collective-permute-start | bytes 3080 | tf_op jit(solution)/shard_map/ppermute | solution.py:31
  1263.1 41.3 %collective-permute-start.216 = (f32[2,64]{0,1:T(8,128)S(1)}, f32[2,64]{0,1:T(8,128)S(1)}, u32[]{:S(2)}, u32[]{:S(2)}) collective-permute-start(f32[2,64]{0,1:T(8,128)S(1)} %copy.3564), channel_id=1, source_target_pairs={{0,1},{1,2},{2,3},{3,4},{4,5},{5,6},{6,7},{7,0},{8,9},{9,10},{10,1... | collective-permute-start | bytes 1544 | tf_op jit(solution)/shard_map/ppermute | solution.py:26
  1263.1 41.3 %collective-permute-start.217 = (f32[2,64]{0,1:T(8,128)S(1)}, f32[2,64]{0,1:T(8,128)S(1)}, u32[]{:S(2)}, u32[]{:S(2)}) collective-permute-start(f32[2,64]{0,1:T(8,128)S(1)} %copy.3564), channel_id=1, source_target_pairs={{0,7},{1,0},{2,1},{3,2},{4,3},{5,4},{6,5},{7,6},{8,15},{9,8},{10,9... | collective-permute-start | bytes 1544 | tf_op jit(solution)/shard_map/ppermute | solution.py:31
  1374.5 38.6 %collective-permute-start.233 = (f32[2,64]{0,1:T(8,128)S(1)}, f32[2,64]{0,1:T(8,128)S(1)}, u32[]{:S(2)}, u32[]{:S(2)}) collective-permute-start(f32[2,64]{0,1:T(8,128)S(1)} %copy.3592), channel_id=1, source_target_pairs={{0,1},{1,2},{2,3},{3,4},{4,5},{5,6},{6,7},{7,0},{8,9},{9,10},{10,1... | collective-permute-start | bytes 1544 | tf_op jit(solution)/shard_map/ppermute | solution.py:26
  1374.5 38.6 %collective-permute-start.234 = (f32[2,64]{0,1:T(8,128)S(1)}, f32[2,64]{0,1:T(8,128)S(1)}, u32[]{:S(2)}, u32[]{:S(2)}) collective-permute-start(f32[2,64]{0,1:T(8,128)S(1)} %copy.3592), channel_id=1, source_target_pairs={{0,7},{1,0},{2,1},{3,2},{4,3},{5,4},{6,5},{7,6},{8,15},{9,8},{10,9... | collective-permute-start | bytes 1544 | tf_op jit(solution)/shard_map/ppermute | solution.py:31
  1430.9 31.6 %collective-permute-start.244 = (f32[2,128]{1,0:T(2,128)S(1)}, f32[2,128]{1,0:T(2,128)S(1)}, u32[]{:S(2)}, u32[]{:S(2)}) collective-permute-start(f32[2,128]{1,0:T(2,128)S(1)} %bitcast.420), channel_id=1, source_target_pairs={{0,1},{1,2},{2,3},{3,4},{4,5},{5,6},{6,7},{7,0},{8,9},{9,10},{10,1... | collective-permute-start | bytes 3080 | tf_op jit(solution)/shard_map/ppermute | solution.py:26
  1431.0 32.0 %collective-permute-start.245 = (f32[2,128]{1,0:T(2,128)S(1)}, f32[2,128]{1,0:T(2,128)S(1)}, u32[]{:S(2)}, u32[]{:S(2)}) collective-permute-start(f32[2,128]{1,0:T(2,128)S(1)} %bitcast.421), channel_id=1, source_target_pairs={{0,7},{1,0},{2,1},{3,2},{4,3},{5,4},{6,5},{7,6},{8,15},{9,8},{10,9... | collective-permute-start | bytes 3080 | tf_op jit(solution)/shard_map/ppermute | solution.py:31
  1526.5 22.8 %collective-permute-start.255 = (f32[2,128]{1,0:T(2,128)S(1)}, f32[2,128]{1,0:T(2,128)S(1)}, u32[]{:S(2)}, u32[]{:S(2)}) collective-permute-start(f32[2,128]{1,0:T(2,128)S(1)} %bitcast.384), channel_id=1, source_target_pairs={{0,1},{1,2},{2,3},{3,4},{4,5},{5,6},{6,7},{7,0},{8,9},{9,10},{10,1... | collective-permute-start | bytes 3080 | tf_op jit(solution)/shard_map/ppermute | solution.py:26
  1527.4 22.3 %collective-permute-start.256 = (f32[2,128]{1,0:T(2,128)S(1)}, f32[2,128]{1,0:T(2,128)S(1)}, u32[]{:S(2)}, u32[]{:S(2)}) collective-permute-start(f32[2,128]{1,0:T(2,128)S(1)} %bitcast.385), channel_id=1, source_target_pairs={{0,7},{1,0},{2,1},{3,2},{4,3},{5,4},{6,5},{7,6},{8,15},{9,8},{10,9... | collective-permute-start | bytes 3080 | tf_op jit(solution)/shard_map/ppermute | solution.py:31
  (220 other events, 1879.2 us)
